TPU v7x, 32 devices: a whole 2x2x4 slice. The times are simulated.
32 devices in a mesh: orb: 8 (over z, x), grid: 4 (over y, core).
Axes of the slice: x: 2, y: 2, z: 4, core: 2. Of those that a mesh axis runs over, the one named last changes fastest.
Arguments:
- potentials: float32 [8, 2, 4, 64, 1024], P('orb', None, None, 'grid'), may hold values from -6 to 6
- orbitals: float32 [32, 64, 1024], P('orb', 'grid'), may hold values from -6 to 6
- local_pot: float32 [64, 1024], P('grid'), may hold values from 0 to 1
- shifts: float32 [32], P('orb'), may hold values from 0.75 to 2
- occupation: int32 [32], P('orb'), may hold values from 1 to 2
- owner: int32 [2], replicated, may hold values from 0 to 7
Outputs:
- response: float32 [8, 2, 4, 64, 1024], P('orb', None, None, 'grid')
All inputs are finite; a program needn't handle non-finite values.
Results may differ from a plain program's by a relative error of at most 0.00002.
Values sent between devices are 32-bit elements; how exact they have to be, the bound alone decides.
A program may use at most 64 MiB of HBM per device.

v0:
```python
import jax
import jax.numpy as jnp
from jax import lax
from jax.sharding import PartitionSpec as P

NZ = 32
ITERS = 4


NEAR_COEF = 4.0 / 3.0
FAR_COEF = -1.0 / 12.0
CENTER_COEF = -2.5
KINETIC_DIAG = 3.75


def with_halo(cells, sides, width):
    for axis, dim in sides:
        count = lax.axis_size(axis)
        ends = count - 1
        head = lax.slice_in_dim(cells, 0, width, axis=dim)
        tail = lax.slice_in_dim(cells, cells.shape[dim] - width, cells.shape[dim], axis=dim)
        cells = jnp.concatenate(
            [
                lax.ppermute(tail, axis, [(i, (i + 1) % count) for i in range(ends)]),
                cells,
                lax.ppermute(head, axis, [((i + 1) % count, i) for i in range(ends)]),
            ],
            axis=dim,
        )
    return cells


def from_root(value, axis, source):
    kept = jnp.where(lax.axis_index(axis) == source, value, 0).astype(value.dtype)
    return lax.psum(kept, axis)


def laplacian(padded, solution):
    cell_rows = solution.shape[-2]
    plane_cells = solution.shape[-1]
    along_rows = NEAR_COEF * (
        padded[..., 1 : cell_rows + 1, :] + padded[..., 3 : cell_rows + 3, :]
    ) + FAR_COEF * (padded[..., 0:cell_rows, :] + padded[..., 4 : cell_rows + 4, :])
    widths = [(0, 0)] * (solution.ndim - 1)
    padded_cols = jnp.pad(solution, widths + [(2 * NZ, 2 * NZ)])
    along_cols = NEAR_COEF * (
        padded_cols[..., NZ : NZ + plane_cells] + padded_cols[..., 3 * NZ : 3 * NZ + plane_cells]
    ) + FAR_COEF * (
        padded_cols[..., 0:plane_cells] + padded_cols[..., 4 * NZ : 4 * NZ + plane_cells]
    )
    padded_depth = jnp.pad(solution, widths + [(2, 2)])
    z_index = jnp.arange(plane_cells, dtype=jnp.int32) % NZ
    lower_one = (z_index >= 1).astype(solution.dtype)
    upper_one = (z_index <= NZ - 2).astype(solution.dtype)
    lower_two = (z_index >= 2).astype(solution.dtype)
    upper_two = (z_index <= NZ - 3).astype(solution.dtype)
    along_depth = NEAR_COEF * (
        padded_depth[..., 1 : plane_cells + 1] * lower_one
        + padded_depth[..., 3 : plane_cells + 3] * upper_one
    ) + FAR_COEF * (
        padded_depth[..., 0:plane_cells] * lower_two
        + padded_depth[..., 4 : plane_cells + 4] * upper_two
    )
    return along_rows + along_cols + along_depth + 3.0 * CENTER_COEF * solution


def sweep(padded, solution, source, potential, diagonal):
    applied = -0.5 * laplacian(padded, solution) + potential * solution
    return solution + (source - applied) / diagonal


def shards(potentials, orbitals, local_pot, shifts, occupation, owner):
    cell_rows = orbitals.shape[1]
    orbital_count = orbitals.shape[0]
    position = lax.axis_index("orb")
    weights = occupation.astype(jnp.float32)
    stored = potentials[0]
    block_count = stored.shape[0]
    results = []
    for block_index in range(block_count):
        trials = from_root(stored[block_index], "orb", owner[block_index])
        halo_depth = 2 * ITERS
        trial_count = trials.shape[0]
        stacked = jnp.concatenate([orbitals, trials, local_pot[None]], axis=0)
        extended = with_halo(stacked, (("grid", 1),), halo_depth)
        orbit_ext = extended[:orbital_count]
        trial_ext = extended[orbital_count : orbital_count + trial_count]
        local_ext = extended[orbital_count + trial_count]
        source_ext = -(trial_ext[None] * orbit_ext[:, None])
        potential_ext = local_ext[None, None] + shifts[:, None, None, None]
        diagonal_ext = KINETIC_DIAG + potential_ext
        global_rows = (
            lax.axis_index("grid") * cell_rows
            - halo_depth
            + jnp.arange(cell_rows + 2 * halo_depth, dtype=jnp.int32)
        )
        inside = ((global_rows >= 0) & (global_rows < cell_rows * lax.axis_size("grid"))).astype(
            jnp.float32
        )[:, None]
        solution_ext = source_ext / diagonal_ext
        for repeat in range(ITERS):
            margin = 2 * (repeat + 1)
            extent = cell_rows + 2 * halo_depth - 2 * margin
            center = solution_ext[:, :, 2 : 2 + extent]
            source_cut = source_ext[:, :, margin : margin + extent]
            potential_cut = potential_ext[:, :, margin : margin + extent]
            diagonal_cut = diagonal_ext[:, :, margin : margin + extent]
            inside_cut = inside[margin : margin + extent]
            solution_ext = (
                sweep(solution_ext, center, source_cut, potential_cut, diagonal_cut) * inside_cut
            )
        results.append(
            lax.psum(
                jnp.sum(weights[:, None, None, None] * orbitals[:, None] * solution_ext, axis=0),
                "orb",
            )
        )
    totals = jnp.stack(results, 0)
    owned = (owner == position).astype(jnp.float32)
    return (owned[:, None, None, None] * totals)[None]


def solution(mesh):
    in_specs = (
        P("orb", None, None, "grid", None),
        P("orb", "grid", None),
        P("grid", None),
        P("orb"),
        P("orb"),
        P(),
    )
    out_specs = P("orb", None, None, "grid", None)
    return jax.shard_map(shards, mesh=mesh, in_specs=in_specs, out_specs=out_specs, check_vma=False)
```

profile of v0, /device:TPU:0, one launch (start us, length us, event | category | flops | bytes accessed | tf_op | source)
XLA Modules:
  0.0 220.6 jit_solution(12964091721920774921)
XLA Ops:
  6.5 1.4 fusion.225
  9.2 1.9 select_bitcast_fusion.1
  11.1 0.0 all-reduce.23.cloned.1.call-update
  11.1 0.0 all-reduce.21.cloned.1.call-start
  11.1 0.1 slice.471
  11.2 0.1 slice.488
  11.3 0.1 slice.505
  11.4 0.1 slice.522
  11.4 75.5 %all-reduce.23.cloned.1.call-done = (f32[4,16,1024]{2,1,0:T(8,128)}, f32[4,16,1024]{2,1,0:T(8,128)}) async-done(((f32[4,16,1024]{2,1,0:T(8,128)}, f32[4,16,1024]{2,1,0:T(8,128)}), (f32[4,16,1024]{2,1,0:T(8,128)}, f32[4,16,1024]{2,1,0:T(8,128)})) %all-reduce.23.cloned.1.call-update) | async-done | bytes 524304 | tf_op jit(solution)/shard_map/psum | solution.py:35
  87.0 1.2 pad_maximum_fusion.5
  88.2 1.4 collective-permute-start
  89.6 1.3 collective-permute-start.1
  91.0 4.7 %collective-permute-start.2 = (f32[9,8,1024]{2,1,0:T(8,128)S(1)}, f32[9,8,1024]{2,1,0:T(8,128)S(1)}, u32[]{:S(2)}, u32[]{:S(2)}) collective-permute-start(f32[9,8,1024]{2,1,0:T(8,128)S(1)} %get-tuple-element.19), channel_id=1, source_target_pairs={{0,1},{1,2},{2,3},{4,5},{5,6},{6,7},{8,9},{9,10},{10,11},{12,13},{... | collective-permute-start | bytes 884744 | tf_op jit(solution)/shard_map/ppermute | solution.py:24
  95.7 1.3 collective-permute-start.3
  97.0 0.1 broadcast_multiply_fusion
  97.1 0.0 collective-permute-done
  97.2 3.3 %collective-permute-done.3 = f32[9,8,1024]{2,1,0:T(8,128)S(1)} collective-permute-done((f32[9,8,1024]{2,1,0:T(8,128)S(1)}, f32[9,8,1024]{2,1,0:T(8,128)S(1)}, u32[]{:S(2)}, u32[]{:S(2)}) %collective-permute-start.3) | collective-permute-done | bytes 294944 | tf_op jit(solution)/shard_map/ppermute | solution.py:26
  100.4 0.2 fusion.157
  100.7 0.0 copy-start.4
  100.7 0.1 fusion.221
  100.9 0.5 copy-done.4
  101.4 0.2 add_add_fusion.1
  101.5 0.3 broadcast_add_fusion.3
  101.9 0.1 slice_bitcast_fusion.2
  102.0 0.1 slice_bitcast_fusion.3
  102.2 0.1 slice_bitcast_fusion
  102.4 0.1 slice_bitcast_fusion.1
  102.6 0.6 multiply_negate_fusion.1
  103.2 0.4 slice.599
  103.6 4.8 %fusion.51 = f32[4,4,28,1024]{3,2,1,0:T(8,128)S(1)} fusion(f32[4,4,28,1024]{3,2,1,0:T(8,128)S(1)} %slice.599, f32[4,4,32,1024]{3,2,1,0:T(8,128)S(1)} %get-tuple-element.14, f32[4,4,32,1024]{3,2,1,0:T(8,128)S(1)} %get-tuple-element.13, f32[28]{0:T(128)S(1)} %slice.471, f32[4,28,1024]{2,1,0:T(8,128)S(1)} %slice_bitcast_fusion.2, ...), kind=kLoop, calls=%fused_computation.73 | loop fusion | flops 13762560 | bytes 13779056 | tf_op jit(solution)/shard_map/mul | solution.py:110
  108.4 0.2 slice.607
  108.6 3.5 %fusion.155 = f32[4,4,24,1024]{3,2,1,0:T(8,128)S(1)} fusion(f32[4,4,24,1024]{3,2,1,0:T(8,128)S(1)} %slice.607, f32[4,4,28,1024]{3,2,1,0:T(8,128)S(1)} %fusion.51, f32[4,4,32,1024]{3,2,1,0:T(8,128)S(1)} %get-tuple-element.13, f32[24]{0:T(128)S(1)} %slice.488, f32[4,24,1024]{2,1,0:T(8,128)S(1)} %slice_bitcast_fusion.10, ...), kind=kLoop, calls=%fused_computation.219 | loop fusion | flops 11796480 | bytes 11812960 | tf_op jit(solution)/shard_map/mul | solution.py:110
  112.2 0.2 slice.615
  112.4 3.5 %fusion.154 = f32[4,4,20,1024]{3,2,1,0:T(8,128)S(1)} fusion(f32[4,4,20,1024]{3,2,1,0:T(8,128)S(1)} %slice.615, f32[4,4,24,1024]{3,2,1,0:T(8,128)S(1)} %fusion.155, f32[4,4,32,1024]{3,2,1,0:T(8,128)S(1)} %get-tuple-element.13, f32[20]{0:T(128)S(1)} %slice.505, f32[4,20,1024]{2,1,0:T(8,128)S(1)} %slice_bitcast_fusion.8, ...), kind=kLoop, calls=%fused_computation.218 | loop fusion | flops 9830400 | bytes 9846864 | tf_op jit(solution)/shard_map/mul | solution.py:110
  115.9 0.2 slice.623
  116.1 0.6 multiply_negate_fusion
  116.6 0.4 slice.636
  117.1 4.6 %fusion.50 = f32[4,4,28,1024]{3,2,1,0:T(8,128)S(1)} fusion(f32[4,4,28,1024]{3,2,1,0:T(8,128)S(1)} %slice.636, f32[4,4,32,1024]{3,2,1,0:T(8,128)S(1)} %get-tuple-element.16, f32[4,4,32,1024]{3,2,1,0:T(8,128)S(1)} %get-tuple-element.15, f32[4,28,1024]{2,1,0:T(8,128)S(1)} %slice_bitcast_fusion, f32[4,28,1024]{2,1,0:T(8,128)S(1)} %slice_bitcast_fusion.1, ...), kind=kLoop, calls=%fused_computation.72 | loop fusion | flops 13762560 | bytes 13779056 | tf_op jit(solution)/shard_map/mul | solution.py:110
  121.7 0.2 slice.644
  121.9 3.5 %fusion.153 = f32[4,4,24,1024]{3,2,1,0:T(8,128)S(1)} fusion(f32[4,4,24,1024]{3,2,1,0:T(8,128)S(1)} %slice.644, f32[4,4,28,1024]{3,2,1,0:T(8,128)S(1)} %fusion.50, f32[4,4,32,1024]{3,2,1,0:T(8,128)S(1)} %get-tuple-element.15, f32[4,24,1024]{2,1,0:T(8,128)S(1)} %slice_bitcast_fusion.6, f32[4,24,1024]{2,1,0:T(8,128)S(1)} %slice_bitcast_fusion.7, ...), kind=kLoop, calls=%fused_computation.217 | loop fusion | flops 11796480 | bytes 11812960 | tf_op jit(solution)/shard_map/mul | solution.py:110
  125.4 0.3 slice.652
  125.7 3.7 %fusion.152 = f32[4,4,20,1024]{3,2,1,0:T(8,128)S(1)} fusion(f32[4,4,20,1024]{3,2,1,0:T(8,128)S(1)} %slice.652, f32[4,4,24,1024]{3,2,1,0:T(8,128)S(1)} %fusion.153, f32[4,4,32,1024]{3,2,1,0:T(8,128)S(1)} %get-tuple-element.15, f32[4,20,1024]{2,1,0:T(8,128)S(1)} %slice_bitcast_fusion.4, f32[4,20,1024]{2,1,0:T(8,128)S(1)} %slice_bitcast_fusion.5, ...), kind=kLoop, calls=%fused_computation.216 | loop fusion | flops 9830400 | bytes 9846864 | tf_op jit(solution)/shard_map/mul | solution.py:110
  129.4 0.1 slice.660
  129.5 3.1 %multiply_reduce_fusion.1 = f32[4,16,1024]{2,1,0:T(8,128)} fusion(f32[4,4,16,1024]{3,2,1,0:T(8,128)S(1)} %slice.623, f32[4,4,20,1024]{3,2,1,0:T(8,128)S(1)} %fusion.154, f32[4,4,32,1024]{3,2,1,0:T(8,128)S(1)} %get-tuple-element.13, f32[16]{0:T(128)S(1)} %slice.522, f32[4,16,1024]{2,1,0:T(8,128)S(1)} %slice_bitcast_fusion.14, ...), kind=kLoop, calls=%fused_computation.298 | loop fusion | flops 8323072 | bytes 7356480 | tf_op jit(solution)/shard_map/reduce_sum | solution.py:114
  132.7 3.1 %multiply_reduce_fusion = f32[4,16,1024]{2,1,0:T(8,128)} fusion(f32[4,4,16,1024]{3,2,1,0:T(8,128)S(1)} %slice.660, f32[4,4,20,1024]{3,2,1,0:T(8,128)S(1)} %fusion.152, f32[4,4,32,1024]{3,2,1,0:T(8,128)S(1)} %get-tuple-element.15, f32[4,16,1024]{2,1,0:T(8,128)S(1)} %slice_bitcast_fusion.12, f32[4,16,1024]{2,1,0:T(8,128)S(1)} %slice_bitcast_fusion.13, ...), kind=kLoop, calls=%fused_computation.296 | loop fusion | flops 8323072 | bytes 7356480 | tf_op jit(solution)/shard_map/reduce_sum | solution.py:114
  135.8 0.0 all-reduce.21.cloned.1.call-update
  135.8 76.0 %all-reduce.21.cloned.1.call-done = (f32[1,1,4,16,1024]{4,3,2,1,0:T(8,128)}, f32[1,1,4,16,1024]{4,3,2,1,0:T(8,128)}) async-done(((f32[1,1,4,16,1024]{4,3,2,1,0:T(8,128)}, f32[1,1,4,16,1024]{4,3,2,1,0:T(8,128)}), (f32[1,1,4,16,1024]{4,3,2,1,0:T(8,128)}, f32[1,1,4,16,1024]{4,3,2,1,0:T(8,128)})) %all-reduce.21.cloned.1.call-update) | async-done | bytes 524304 | tf_op jit(solution)/shard_map/psum | solution.py:113
  211.8 1.9 maximum_multiply_fusion
  (35 shorter events, 0.5 us)
Async XLA Ops:
  6.5 4.9 %copy-start.6 = (s32[4]{0:T(128)S(1)}, s32[4]{0:T(128)}, u32[]{:S(2)}) copy-start(s32[4]{0:T(128)} %param.10) | copy-start | bytes 52
  6.5 80.4 %copy-start.3 = (f32[16,1024]{1,0:T(8,128)S(1)}, f32[16,1024]{1,0:T(8,128)}, u32[]{:S(2)}) copy-start(f32[16,1024]{1,0:T(8,128)} %param.8) | copy-start | bytes 196612
  6.5 80.4 %copy-start = (f32[4,16,1024]{2,1,0:T(8,128)S(1)}, f32[4,16,1024]{2,1,0:T(8,128)}, u32[]{:S(2)}) copy-start(f32[4,16,1024]{2,1,0:T(8,128)} %param.7) | copy-start | bytes 786436
  6.5 80.4 %all-reduce.23.cloned.1.call-start = ((), (), s32[]{:S(2)}) async-start(), calls=%async_computation.1 | async-start | bytes 1048576 | tf_op jit(solution)/shard_map/psum | solution.py:35
  11.1 200.8 %all-reduce.21.cloned.1.call-start = ((), (), s32[]{:S(2)}) async-start(), calls=%async_computation | async-start | bytes 1048576 | tf_op jit(solution)/shard_map/psum | solution.py:113
  88.1 12.3 %copy-start.1 = (f32[4,16,1024]{2,1,0:T(8,128)S(1)}, f32[4,16,1024]{2,1,0:T(8,128)}, u32[]{:S(2)}) copy-start(f32[4,16,1024]{2,1,0:T(8,128)} %get-tuple-element.7) | copy-start | bytes 786436
  88.1 12.3 %copy-start.2 = (f32[4,16,1024]{2,1,0:T(8,128)S(1)}, f32[4,16,1024]{2,1,0:T(8,128)}, u32[]{:S(2)}) copy-start(f32[4,16,1024]{2,1,0:T(8,128)} %get-tuple-element.8) | copy-start | bytes 786436
  88.2 9.0 %collective-permute-start = (f32[9,8,1024]{2,1,0:T(8,128)S(1)}, f32[9,8,1024]{2,1,0:T(8,128)S(1)}, u32[]{:S(2)}, u32[]{:S(2)}) collective-permute-start(f32[9,8,1024]{2,1,0:T(8,128)S(1)} %get-tuple-element.17), channel_id=1, source_target_pairs={{0,1},{1,2},{2,3},{4,5},{5,6},{6,7},{8,9},{9,10},{10,11},{12,13},{... | collective-permute-start | bytes 884744 | tf_op jit(solution)/shard_map/ppermute | solution.py:24
  89.6 7.5 %collective-permute-start.1 = (f32[9,8,1024]{2,1,0:T(8,128)S(1)}, f32[9,8,1024]{2,1,0:T(8,128)S(1)}, u32[]{:S(2)}, u32[]{:S(2)}) collective-permute-start(f32[9,8,1024]{2,1,0:T(8,128)S(1)} %get-tuple-element.18), channel_id=1, source_target_pairs={{1,0},{2,1},{3,2},{5,4},{6,5},{7,6},{9,8},{10,9},{11,10},{13,12},{... | collective-permute-start | bytes 884744 | tf_op jit(solution)/shard_map/ppermute | solution.py:26
  91.0 6.2 %collective-permute-start.2 = (f32[9,8,1024]{2,1,0:T(8,128)S(1)}, f32[9,8,1024]{2,1,0:T(8,128)S(1)}, u32[]{:S(2)}, u32[]{:S(2)}) collective-permute-start(f32[9,8,1024]{2,1,0:T(8,128)S(1)} %get-tuple-element.19), channel_id=1, source_target_pairs={{0,1},{1,2},{2,3},{4,5},{5,6},{6,7},{8,9},{9,10},{10,11},{12,13},{... | collective-permute-start | bytes 884744 | tf_op jit(solution)/shard_map/ppermute | solution.py:24
  95.7 4.7 %collective-permute-start.3 = (f32[9,8,1024]{2,1,0:T(8,128)S(1)}, f32[9,8,1024]{2,1,0:T(8,128)S(1)}, u32[]{:S(2)}, u32[]{:S(2)}) collective-permute-start(f32[9,8,1024]{2,1,0:T(8,128)S(1)} %get-tuple-element.20), channel_id=1, source_target_pairs={{1,0},{2,1},{3,2},{5,4},{6,5},{7,6},{9,8},{10,9},{11,10},{13,12},{... | collective-permute-start | bytes 884744 | tf_op jit(solution)/shard_map/ppermute | solution.py:26
  100.7 0.7 copy-start.4
  132.7 3.1 %copy-start.5 = (s32[2]{0:T(128)S(1)}, s32[2]{0:T(128)}, u32[]{:S(2)}) copy-start(s32[2]{0:T(128)} %param.11) | copy-start | bytes 28
Sparse Core Ops, SparseCore 0:
  11.2 75.7 all-reduce.22
  135.9 75.8 all-reduce.20
where the time goes:
time: 221 us
  waiting for transfers between devices  155 us (70%)
  other arithmetic  36.9 us (17%)
  between operations  15.1 us (7%)
  starting transfers between devices  8.81 us (4%)
  local copies, waits for them, and re-layouts  5.03 us (2%)
    psum x1, waiting for transfers between devices, shards(): lax.psum(jnp.sum(weights[:, None, None, None] * orbitals[:, None] * solut...  76 us
    psum x1, waiting for transfers between devices, from_root(): return lax.psum(kept, axis)  75.5 us
    mul x6, other arithmetic, shards(): sweep(solution_ext, center, source_cut, potential_cut, diagonal_cut)  23.7 us
    reduce_sum x2, other arithmetic, shards(): jnp.sum(weights[:, None, None, None] * orbitals[:, None] * solution_ext,...  6.25 us
    ppermute x2, starting transfers between devices, with_halo(): lax.ppermute(tail, axis, [(i, (i + 1) % count) for i in range(ends)])  6.18 us
  transfers between devices with their start and end apart: 6, of which 3 were waited for; matrix products, arithmetic and copies ran while one was open for 0% of the time, Pallas kernels for 0%

commit v1 on v0

v1 whole, which is shorter than its diff:
```python
import functools

import jax
import jax.numpy as jnp
from jax import lax
from jax.experimental import pallas as pl
from jax.experimental.pallas import tpu as pltpu
from jax.sharding import PartitionSpec as P

NZ = 32
ITERS = 4
REACH = 2
HALO = REACH * ITERS
KINETIC_DIAG = 3.75
PAIR = 2
MESH = pl.DeviceIdType.MESH


class Ring:
    def __init__(self, count, grids):
        self.count, self.lines, self.grids = count, count // PAIR, grids
        self.me = lax.axis_index("orb")
        self.row = lax.axis_index("grid")
        self.line, self.side = self.me // PAIR, self.me % PAIR
        self.partner = self.line * PAIR + (1 - self.side)

    def peer(self, step):
        return (self.line + step) % self.lines

    def at_line(self, line):
        return {"orb": line * PAIR + self.side, "grid": self.row}

    def across(self):
        return {"orb": self.partner, "grid": self.row}

    def up(self):
        return {"orb": self.me, "grid": self.row - 1}

    def down(self):
        return {"orb": self.me, "grid": self.row + 1}


def enter(ring, with_grid):
    barrier = pltpu.get_barrier_semaphore()
    pl.semaphore_signal(barrier, inc=1, device_id=ring.across(), device_id_type=MESH)
    for step in range(1, ring.lines):
        target = ring.at_line(ring.peer(step))
        pl.semaphore_signal(barrier, inc=1, device_id=target, device_id_type=MESH)
    if with_grid:

        @pl.when(ring.row > 0)
        def _():
            pl.semaphore_signal(barrier, inc=1, device_id=ring.up(), device_id_type=MESH)

        @pl.when(ring.row < ring.grids - 1)
        def _():
            pl.semaphore_signal(barrier, inc=1, device_id=ring.down(), device_id_type=MESH)

    peers = ring.lines
    if with_grid:
        last = ring.grids - 1
        peers = peers + (ring.row + last) // ring.grids + (2 * last - ring.row) // ring.grids
    pl.semaphore_wait(barrier, peers)


def piece(ref, count, index, start, rows):
    split = count // ref.shape[0]
    if split == 1:
        return ref.at[index, pl.ds(start, rows)]
    width = ref.shape[2] // split
    lane = pl.multiple_of((index % split) * width, 128)
    return ref.at[index // split, pl.ds(start, rows), pl.ds(lane, width)]


def send(src, dst, send_sem, recv_sem, target):
    return pltpu.make_async_remote_copy(
        src_ref=src, dst_ref=dst, send_sem=send_sem, recv_sem=recv_sem,
        device_id=target, device_id_type=MESH,
    )


def start_cross(ring, data, crossed, sems, rows):
    copies = []
    for step in list(range(1, ring.lines)) + [0]:
        line = ring.peer(step)
        src = piece(data, ring.count, line * PAIR + (1 - ring.side), 0, rows)
        copy = send(src, crossed.at[line], sems.at[0, line], sems.at[1, line], ring.across())
        copy.start()
        copies.append((step, copy))
    return copies


def line_scatter(ring, data, crossed, merged, gathered, copies, sems, rows, merge):
    sent = []
    for step, copy in copies:
        line = ring.peer(step)
        copy.wait_recv()
        mine = piece(data, ring.count, line * PAIR + ring.side, 0, rows)[...]
        value = merge(line * PAIR + ring.side, mine, crossed[line])
        if step == 0:
            gathered[ring.line] = value
        else:
            merged[step] = value
            out = send(
                merged.at[step], gathered.at[ring.line],
                sems.at[0, line], sems.at[1, ring.line], ring.at_line(line),
            )
            out.start()
            sent.append((line, out))
    for line, out in sent:
        send(
            merged.at[1], gathered.at[line], sems.at[0, line], sems.at[1, line], ring.at_line(line)
        ).wait_recv()
    return sent


def line_gather(ring, full, start, rows, line_sems, side_sems, arrived):
    own = piece(full, ring.count, ring.me, start, rows)
    sent = []
    for step in range(1, ring.lines):
        line = ring.peer(step)
        out = send(own, own, line_sems.at[0, line], line_sems.at[1, ring.line], ring.at_line(line))
        out.start()
        sent.append(out)
    out = send(
        own, own, side_sems.at[0, ring.line], side_sems.at[1, ring.line], ring.across()
    )
    out.start()
    sent.append(out)
    arrived(ring.me)
    for step in range(1, ring.lines):
        line = ring.peer(step)
        part = piece(full, ring.count, line * PAIR + ring.side, start, rows)
        send(part, part, line_sems.at[0, line], line_sems.at[1, line], ring.at_line(line)).wait_recv()
        out = send(part, part, side_sems.at[0, line], side_sems.at[1, line], ring.across())
        out.start()
        sent.append(out)
        arrived(line * PAIR + ring.side)
    for step in range(ring.lines):
        line = ring.peer(step)
        index = line * PAIR + (1 - ring.side)
        part = piece(full, ring.count, index, start, rows)
        send(part, part, side_sems.at[0, line], side_sems.at[1, line], ring.across()).wait_recv()
        arrived(index)
    return sent


def spread_kernel(
    count, grids, blocks, owner_ref, pot_ref, orb_ref, local_ref, trial_out, orb_out, local_out,
    crossed, merged, gathered, cross_sems, scatter_sems, line_sems, side_sems, halo_sems, edge_sems,
):
    ring = Ring(count, grids)
    rows = orb_ref.shape[1]
    last = HALO + rows
    per_block = count // blocks
    enter(ring, True)
    copies = start_cross(ring, pot_ref, crossed, cross_sems, rows)
    has_up, has_down = ring.row > 0, ring.row < grids - 1

    def edge_up(make):
        return [
            make(orb_ref.at[:, pl.ds(0, HALO)], orb_out.at[:, pl.ds(last, HALO)], 0),
            make(local_ref.at[pl.ds(0, HALO)], local_out.at[pl.ds(last, HALO)], 1),
        ]

    def edge_down(make):
        return [
            make(orb_ref.at[:, pl.ds(rows - HALO, HALO)], orb_out.at[:, pl.ds(0, HALO)], 2),
            make(local_ref.at[pl.ds(rows - HALO, HALO)], local_out.at[pl.ds(0, HALO)], 3),
        ]

    def edge(target):
        return lambda src, dst, k: send(src, dst, edge_sems.at[0, k], edge_sems.at[1, k], target)

    @pl.when(has_up)
    def _():
        for copy in edge_up(edge(ring.up())):
            copy.start()

    @pl.when(has_down)
    def _():
        for copy in edge_down(edge(ring.down())):
            copy.start()

    orb_out[:, HALO:last] = orb_ref[...]
    local_out[HALO:last] = local_ref[...]

    @pl.when(jnp.logical_not(has_up))
    def _():
        orb_out[:, 0:HALO] = jnp.zeros((orb_ref.shape[0], HALO, orb_ref.shape[2]), jnp.float32)
        local_out[0:HALO] = jnp.zeros((HALO, orb_ref.shape[2]), jnp.float32)
        trial_out[:, 0:HALO] = jnp.zeros((pot_ref.shape[0], HALO, orb_ref.shape[2]), jnp.float32)

    @pl.when(jnp.logical_not(has_down))
    def _():
        orb_out[:, last:] = jnp.zeros((orb_ref.shape[0], HALO, orb_ref.shape[2]), jnp.float32)
        local_out[last:] = jnp.zeros((HALO, orb_ref.shape[2]), jnp.float32)
        trial_out[:, last:] = jnp.zeros((pot_ref.shape[0], HALO, orb_ref.shape[2]), jnp.float32)

    def choose(index, mine, other):
        return jnp.where(owner_ref[index // per_block] == ring.partner, other, mine)

    sent = line_scatter(
        ring, pot_ref, crossed, merged, gathered, copies, scatter_sems, rows, choose
    )
    piece(trial_out, count, ring.me, HALO, rows)[...] = gathered[
        owner_ref[ring.me // per_block] // PAIR
    ]

    def halo_up(index):
        return send(
            piece(trial_out, count, index, HALO, HALO), piece(trial_out, count, index, last, HALO),
            halo_sems.at[0, 0, index], halo_sems.at[1, 0, index], ring.up(),
        )

    def halo_down(index):
        return send(
            piece(trial_out, count, index, rows, HALO), piece(trial_out, count, index, 0, HALO),
            halo_sems.at[0, 1, index], halo_sems.at[1, 1, index], ring.down(),
        )

    def arrived(index):
        @pl.when(has_up)
        def _():
            halo_up(index).start()

        @pl.when(has_down)
        def _():
            halo_down(index).start()

    more = line_gather(ring, trial_out, HALO, rows, line_sems, side_sems, arrived)

    @pl.when(has_up)
    def _():
        for copy in edge_up(edge(ring.up())):
            copy.wait_send()
        for copy in edge_down(edge(ring.up())):
            copy.wait_recv()
        for index in range(count):
            halo_up(index).wait_send()
            halo_down(index).wait_recv()

    @pl.when(has_down)
    def _():
        for copy in edge_down(edge(ring.down())):
            copy.wait_send()
        for copy in edge_up(edge(ring.down())):
            copy.wait_recv()
        for index in range(count):
            halo_down(index).wait_send()
            halo_up(index).wait_recv()

    for step, copy in copies:
        copy.wait_send()
    for line, copy in sent:
        copy.wait_send()
    for copy in more:
        copy.wait_send()


def total_kernel(
    count, grids, part_ref, out_ref,
    crossed, merged, gathered, cross_sems, scatter_sems, line_sems, side_sems,
):
    ring = Ring(count, grids)
    rows = part_ref.shape[1]
    enter(ring, False)
    copies = start_cross(ring, part_ref, crossed, cross_sems, rows)
    sent = line_scatter(
        ring, part_ref, crossed, merged, gathered, copies, scatter_sems, rows,
        lambda index, mine, other: mine + other,
    )
    total = gathered[0]
    for line in range(1, ring.lines):
        total = total + gathered[line]
    piece(out_ref, count, ring.me, 0, rows)[...] = total
    more = line_gather(ring, out_ref, 0, rows, line_sems, side_sems, lambda index: None)
    for step, copy in copies:
        copy.wait_send()
    for line, copy in sent:
        copy.wait_send()
    for copy in more:
        copy.wait_send()


def band_matrix(depth, width):
    k = lax.broadcasted_iota(jnp.int32, (depth, width), 0)
    n = lax.broadcasted_iota(jnp.int32, (depth, width), 1) + width // 2
    far_y, far_z = jnp.abs(k // NZ - n // NZ), jnp.abs(k % NZ - n % NZ)
    near = ((far_y == 1) & (far_z == 0)) | ((far_y == 0) & (far_z == 1))
    far = ((far_y == 2) & (far_z == 0)) | ((far_y == 0) & (far_z == 2))
    return jnp.where(near, 16.0, jnp.where(far, -1.0, 0.0)).astype(jnp.bfloat16)


WIDTH = 256


def sweep_kernel(
    grids, shift_ref, weight_ref, trial_ref, orb_ref, local_ref, out_ref,
    trials, first, scale, now_a, now_b, hi_a, hi_b, lo_a, lo_b, product, density, band, inverse,
):
    n = pl.program_id(0)
    batch, planes, cells = trial_ref.shape
    rows = planes - 2 * HALO

    @pl.when(n == 0)
    def _():
        band[...] = band_matrix(2 * WIDTH, WIDTH)
        density[...] = jnp.zeros_like(density)
        for x in range(planes):
            trials[x] = trial_ref[:, x, :]

    place = lax.axis_index("grid") * rows - HALO
    where = lax.broadcasted_iota(jnp.int32, (planes, cells), 0) + place
    inside = (where >= 0) & (where < rows * grids)
    diagonal = KINETIC_DIAG + (local_ref[...] + shift_ref[n])
    inverse[...] = jnp.where(inside, 1.0 / diagonal, 0.0)

    def split(value):
        high = value.astype(jnp.bfloat16)
        return high, (value - high.astype(jnp.float32)).astype(jnp.bfloat16)

    for x in range(0, planes, 2):
        values = []
        for p in (x, x + 1):
            inv = jnp.broadcast_to(inverse[pl.ds(p, 1), :], (batch, cells))
            orb = jnp.broadcast_to(orb_ref[n, pl.ds(p, 1), :], (batch, cells))
            scale[p] = inv * (1.0 / 24.0)
            value = -(trials[p] * orb) * inv
            first[p] = value
            values.append(value)
        high, low = split(jnp.concatenate(values, axis=0))
        hi_a[x * batch : (x + 2) * batch] = high
        lo_a[x * batch : (x + 2) * batch] = low

    weight = weight_ref[n].astype(jnp.float32)
    current = first
    buffers = ((now_a, hi_a, lo_a), (now_b, hi_b, lo_b))
    for repeat in range(ITERS):
        hi_in, lo_in = buffers[repeat % 2][1:]
        target, hi_out, lo_out = buffers[(repeat + 1) % 2]
        margin = REACH * (repeat + 1)
        extent = planes - 2 * margin
        for left in range(0, cells, WIDTH):
            a = max(0, left - WIDTH // 2)
            b = min(cells, left + WIDTH + WIDTH // 2)
            k = a - (left - WIDTH // 2)
            weights = band[k : k + b - a, :]
            span = slice(margin * batch, (margin + extent) * batch)
            product[0 : extent * batch] = jnp.dot(
                hi_in[span, a:b], weights, preferred_element_type=jnp.float32
            ) + jnp.dot(lo_in[span, a:b], weights, preferred_element_type=jnp.float32)
            lanes = slice(left, left + WIDTH)
            for x in range(margin, margin + extent, 2):
                values = []
                for p in (x, x + 1):
                    near = current[p - 1, :, lanes] + current[p + 1, :, lanes]
                    far = current[p - 2, :, lanes] + current[p + 2, :, lanes]
                    spot = (p - margin) * batch
                    moved = product[spot : spot + batch] + (16.0 * near - far)
                    value = first[p, :, lanes] + scale[p, :, lanes] * moved
                    if repeat == ITERS - 1:
                        orb = weight * orb_ref[n, pl.ds(p, 1), lanes]
                        density[p - margin, :, lanes] += orb * value
                    else:
                        target[p, :, lanes] = value
                        values.append(value)
                if values:
                    high, low = split(jnp.concatenate(values, axis=0))
                    hi_out[x * batch : (x + 2) * batch, lanes] = high
                    lo_out[x * batch : (x + 2) * batch, lanes] = low
        current = target

    @pl.when(n == pl.num_programs(0) - 1)
    def _():
        for x in range(rows):
            out_ref[:, x, :] = density[x]


def shards(count, grids, potentials, orbitals, local_pot, shifts, occupation, owner):
    _, blocks, kinds, rows, cells = potentials.shape
    batch = blocks * kinds
    orbital_count = orbitals.shape[0]
    lines = count // PAIR
    planes = rows + 2 * HALO
    stored = potentials.reshape(batch, rows, cells)
    part = (rows, cells * batch // count)
    vmem = pl.BlockSpec(memory_space=pltpu.VMEM)
    smem = pl.BlockSpec(memory_space=pltpu.SMEM)
    f32 = jnp.float32
    dma = pltpu.SemaphoreType.DMA
    moving = [
        pltpu.VMEM((lines,) + part, f32),
        pltpu.VMEM((lines,) + part, f32),
        pltpu.VMEM((lines,) + part, f32),
        dma((2, lines)), dma((2, lines)), dma((2, lines)), dma((2, lines)),
    ]
    trials, orbs, local = pl.pallas_call(
        functools.partial(spread_kernel, count, grids, blocks),
        out_shape=[
            jax.ShapeDtypeStruct((batch, planes, cells), f32),
            jax.ShapeDtypeStruct((orbital_count, planes, cells), f32),
            jax.ShapeDtypeStruct((planes, cells), f32),
        ],
        in_specs=[smem, vmem, vmem, vmem],
        out_specs=[vmem] * 3,
        scratch_shapes=moving + [dma((2, 2, count)), dma((2, 4))],
        compiler_params=pltpu.CompilerParams(collective_id=0, has_side_effects=True),
        name="spread",
    )(owner, stored, orbitals, local_pot)

    big = pltpu.VMEM((planes, batch, cells), f32)
    half = pltpu.VMEM((planes * batch, cells), jnp.bfloat16)
    partial = pl.pallas_call(
        functools.partial(sweep_kernel, grids),
        out_shape=jax.ShapeDtypeStruct((batch, rows, cells), f32),
        grid=(orbital_count,),
        in_specs=[smem, smem, vmem, vmem, vmem],
        out_specs=vmem,
        scratch_shapes=[big, big, big, big, big, half, half, half, half]
        + [
            pltpu.VMEM((planes * batch, WIDTH), f32),
            pltpu.VMEM((rows, batch, cells), f32),
            pltpu.VMEM((2 * WIDTH, WIDTH), jnp.bfloat16),
            pltpu.VMEM((planes, cells), f32),
        ],
        compiler_params=pltpu.CompilerParams(dimension_semantics=("arbitrary",)),
        name="sweeps",
    )(shifts, occupation, trials, orbs, local)

    totals = pl.pallas_call(
        functools.partial(total_kernel, count, grids),
        out_shape=jax.ShapeDtypeStruct((batch, rows, cells), f32),
        in_specs=[vmem],
        out_specs=vmem,
        scratch_shapes=moving,
        compiler_params=pltpu.CompilerParams(collective_id=1, has_side_effects=True),
        name="total",
    )(partial)
    owned = (owner == lax.axis_index("orb"))[:, None, None, None]
    return jnp.where(owned, totals.reshape(blocks, kinds, rows, cells), 0.0)[None]


def solution(mesh):
    in_specs = (
        P("orb", None, None, "grid", None),
        P("orb", "grid", None),
        P("grid", None),
        P("orb"),
        P("orb"),
        P(),
    )
    out_specs = P("orb", None, None, "grid", None)
    body = functools.partial(shards, mesh.shape["orb"], mesh.shape["grid"])
    return jax.shard_map(body, mesh=mesh, in_specs=in_specs, out_specs=out_specs, check_vma=False)
```

time: 221 us -> 70.5 us (0.32)
  waiting for transfers between devices: 155 us -> 0 us
  Pallas kernels: 0 us -> 67.6 us
  other arithmetic: 36.9 us -> 1.96 us
  between operations: 15.1 us -> 0.03 us
  starting transfers between devices: 8.81 us -> 0 us
  local copies, waits for them, and re-layouts: 5.03 us -> 0.65 us
    psum x2 -> x0, waiting for transfers between devices: 151 us -> none  [the longest x1 76 us: shards(): lax.psum(jnp.sum(weights[:, None, None, None] * orbitals[:, None] * solut...]
    pallas_call x0 -> x3, Pallas kernels: none -> 67.6 us  [the longest x1 29.1 us: shards(): pl.pallas_call(functools.partial(spread_kernel, count, grids, blocks), ou...]
    mul x8 -> x0, other arithmetic: 25.7 us -> none  [the longest x6 23.7 us: shards(): sweep(solution_ext, center, source_cut, potential_cut, diagonal_cut)]
    ppermute x4 -> x0, starting transfers between devices: 8.76 us -> none  [the longest x2 6.18 us: with_halo(): lax.ppermute(tail, axis, [(i, (i + 1) % count) for i in range(ends)])]
    reduce_sum x2 -> x0, other arithmetic: 6.25 us -> none  [shards(): jnp.sum(weights[:, None, None, None] * orbitals[:, None] * solution_ext,...]
    slice x16 -> x0, local copies, waits for them, and re-layouts: 3.85 us -> none  [the longest x8 1.97 us: shards(): center = solution_ext[:, :, 2:2 + extent]]
    ppermute x4 -> x0, waiting for transfers between devices: 3.27 us -> none  [the longest x2 3.27 us: with_halo(): lax.ppermute(head, axis, [((i + 1) % count, i) for i in range(ends)])]
  transfers between devices with their start and end apart: 6 -> 0, of which waited for: 3 -> 0; matrix products, arithmetic and copies ran while one was open for 0% -> 0% of each run, Pallas kernels for 0% -> 0%
where the time goes in v1:
time: 70.5 us; the launch traced here: 70.3 us
  Pallas kernels  67.6 us (96%)
  other arithmetic  1.96 us (3%)
    pallas_call x1, Pallas kernels, shards(): pl.pallas_call(functools.partial(spread_kernel, count, grids, blocks), ou...  29.1 us
    pallas_call x1, Pallas kernels, shards(): pl.pallas_call(functools.partial(total_kernel, count, grids), out_shape=j...  26.9 us
    pallas_call x1, Pallas kernels, shards(): pl.pallas_call(functools.partial(sweep_kernel, grids), out_shape=jax.Shap...  11.6 us
    select_n x1, other arithmetic, shards(): jnp.where(owned, totals.reshape(blocks, kinds, rows, cells), 0.0)[None]  1.95 us

profile of v1, /device:TPU:0, one launch (start us, length us, event | category | flops | bytes accessed | tf_op | source)
XLA Modules:
  0.0 70.3 jit_solution(13829361912342594425)
XLA Ops:
  0.0 29.1 %spread.1 = (f32[8,32,1024]{2,1,0:T(8,128)}, f32[4,32,1024]{2,1,0:T(8,128)}, f32[32,1024]{1,0:T(8,128)}) custom-call(s32[2]{0:T(128)} %owner_ref.1, f32[8,16,1024]{2,1,0:T(8,128)} %bitcast.3, f32[4,16,1024]{2,1,0:T(8,128)} %orb_ref.1, f32[16,1024]{1,0:T(8,128)} %local_ref.1), custom_call_target="tpu_custom_call" | custom-call | tf_op jit(solution)/shard_map/spread/pallas_call | solution.py:398
  29.1 11.6 %sweeps.1.part_ref = f32[8,16,1024]{2,1,0:T(8,128)} custom-call(f32[4]{0:T(128)} %shift_ref.1, s32[4]{0:T(128)} %weight_ref.1, f32[8,32,1024]{2,1,0:T(8,128)} %get-tuple-element.8.trial_ref, f32[4,32,1024]{2,1,0:T(8,128)} %get-tuple-element.9.orb_ref, f32[32,1024]{1,0:T(8,128)} %get-tuple-element.10.local_ref), custom_call_target="tpu_custom_call" | custom-call | tf_op jit(solution)/shard_map/sweeps/pallas_call | solution.py:414
  40.7 26.9 %total.1 = f32[8,16,1024]{2,1,0:T(8,128)} custom-call(f32[8,16,1024]{2,1,0:T(8,128)} %sweeps.1.part_ref), custom_call_target="tpu_custom_call" | custom-call | tf_op jit(solution)/shard_map/total/pallas_call | solution.py:431
  67.6 0.0 copy-start
  67.7 0.6 copy-done
  68.3 2.0 %broadcast_select_fusion = f32[1,2,4,16,1024]{4,3,2,1,0:T(8,128)} fusion(f32[1,2,4,16,1024]{4,3,2,1,0:T(8,128)} %bitcast.2, pred[2]{0:T(512)(128)(4,1)S(1)} %broadcast_compare_fusion), kind=kLoop, calls=%fused_computation | loop fusion | flops 131072 | bytes 1048578 | tf_op jit(solution)/shard_map/jit(_where)/select_n | solution.py:441
  (1 shorter events, 0.0 us)
Async XLA Ops:
  67.6 0.7 copy-start

commit v2 on v1

v2 whole, which is shorter than its diff:
```python
import functools

import jax
import jax.numpy as jnp
from jax import lax
from jax.experimental import pallas as pl
from jax.experimental.pallas import tpu as pltpu
from jax.sharding import PartitionSpec as P

NZ = 32
ITERS = 4
REACH = 2
HALO = REACH * ITERS
KINETIC_DIAG = 3.75
PAIR = 2
MESH = pl.DeviceIdType.MESH


class Ring:
    def __init__(self, count, grids):
        self.count, self.lines, self.grids = count, count // PAIR, grids
        self.me = lax.axis_index("orb")
        self.row = lax.axis_index("grid")
        self.line, self.side = self.me // PAIR, self.me % PAIR
        self.partner = self.line * PAIR + (1 - self.side)

    def peer(self, step):
        return (self.line + step) % self.lines

    def at_line(self, line):
        return {"orb": line * PAIR + self.side, "grid": self.row}

    def across(self):
        return {"orb": self.partner, "grid": self.row}

    def up(self):
        return {"orb": self.me, "grid": self.row - 1}

    def down(self):
        return {"orb": self.me, "grid": self.row + 1}


def enter(ring, with_grid):
    barrier = pltpu.get_barrier_semaphore()
    pl.semaphore_signal(barrier, inc=1, device_id=ring.across(), device_id_type=MESH)
    for step in range(1, ring.lines):
        target = ring.at_line(ring.peer(step))
        pl.semaphore_signal(barrier, inc=1, device_id=target, device_id_type=MESH)
    if with_grid:

        @pl.when(ring.row > 0)
        def _():
            pl.semaphore_signal(barrier, inc=1, device_id=ring.up(), device_id_type=MESH)

        @pl.when(ring.row < ring.grids - 1)
        def _():
            pl.semaphore_signal(barrier, inc=1, device_id=ring.down(), device_id_type=MESH)

    peers = ring.lines
    if with_grid:
        last = ring.grids - 1
        peers = peers + (ring.row + last) // ring.grids + (2 * last - ring.row) // ring.grids
    pl.semaphore_wait(barrier, peers)


def piece(ref, count, index, start, rows):
    split = count // ref.shape[0]
    if split == 1:
        return ref.at[index, pl.ds(start, rows)]
    width = ref.shape[2] // split
    lane = pl.multiple_of((index % split) * width, 128)
    return ref.at[index // split, pl.ds(start, rows), pl.ds(lane, width)]


def send(src, dst, send_sem, recv_sem, target):
    return pltpu.make_async_remote_copy(
        src_ref=src, dst_ref=dst, send_sem=send_sem, recv_sem=recv_sem,
        device_id=target, device_id_type=MESH,
    )


def start_cross(ring, data, crossed, sems, rows):
    copies = []
    for step in list(range(1, ring.lines)) + [0]:
        line = ring.peer(step)
        src = piece(data.at[1 - ring.side], ring.lines, line, 0, rows)
        copy = send(src, crossed.at[line], sems.at[0, line], sems.at[1, line], ring.across())
        copy.start()
        copies.append((step, copy))
    return copies


def line_gather(ring, full, start, rows, sems, arrived):
    own = piece(full, ring.lines, ring.line, start, rows)
    sent = []
    for step in range(1, ring.lines):
        line = ring.peer(step)
        out = send(own, own, sems.at[0, line], sems.at[1, ring.line], ring.at_line(line))
        out.start()
        sent.append(out)
    sent += arrived(ring.line)
    for step in range(1, ring.lines):
        line = ring.peer(ring.lines - step)
        part = piece(full, ring.lines, line, start, rows)
        send(part, part, sems.at[0, line], sems.at[1, line], ring.at_line(line)).wait_recv()
        sent += arrived(line)
    return sent


def spread_kernel(
    count, grids, kinds, owner_ref, shift_ref, weight_ref, pot_ref, orb_ref, local_ref,
    trial_out, orb_out, local_out, pack_out,
    crossed, merged, gathered, cross_sems, scatter_sems, line_sems, halo_sems, edge_sems, pair_sems,
):
    ring = Ring(count, grids)
    orbitals, rows, cells = orb_ref.shape
    half = pot_ref.shape[1]
    split = ring.lines // half
    last = HALO + rows
    has_up, has_down = ring.row > 0, ring.row < grids - 1
    for n in range(orbitals):
        pack_out[0, n] = jnp.full((cells,), shift_ref[n], jnp.float32)
        pack_out[0, orbitals + n] = jnp.full((cells,), weight_ref[n].astype(jnp.float32), jnp.float32)
    enter(ring, True)
    copies = start_cross(ring, pot_ref, crossed, cross_sems, rows)
    center = send(
        orb_ref, orb_out.at[1, :, pl.ds(HALO, rows)],
        pair_sems.at[0, 0], pair_sems.at[1, 0], ring.across(),
    )
    center.start()
    pack = send(
        pack_out.at[0], pack_out.at[1], pair_sems.at[0, 1], pair_sems.at[1, 1], ring.across()
    )
    pack.start()

    def edge_up(target):
        def make(src, dst, k):
            return send(src, dst, edge_sems.at[0, k], edge_sems.at[1, k], target)

        return [
            make(orb_ref.at[:, pl.ds(0, HALO)], orb_out.at[0, :, pl.ds(last, HALO)], 0),
            make(local_ref.at[pl.ds(0, HALO)], local_out.at[pl.ds(last, HALO)], 1),
            make(orb_out.at[1, :, pl.ds(HALO, HALO)], orb_out.at[1, :, pl.ds(last, HALO)], 2),
        ]

    def edge_down(target):
        def make(src, dst, k):
            return send(src, dst, edge_sems.at[0, k], edge_sems.at[1, k], target)

        return [
            make(orb_ref.at[:, pl.ds(rows - HALO, HALO)], orb_out.at[0, :, pl.ds(0, HALO)], 3),
            make(local_ref.at[pl.ds(rows - HALO, HALO)], local_out.at[pl.ds(0, HALO)], 4),
            make(orb_out.at[1, :, pl.ds(rows, HALO)], orb_out.at[1, :, pl.ds(0, HALO)], 5),
        ]

    @pl.when(has_up)
    def _():
        for copy in edge_up(ring.up())[:2]:
            copy.start()

    @pl.when(has_down)
    def _():
        for copy in edge_down(ring.down())[:2]:
            copy.start()

    orb_out[0, :, HALO:last] = orb_ref[...]
    local_out[HALO:last] = local_ref[...]

    def clear(start):
        orb_out[:, :, start : start + HALO] = jnp.zeros((2, orbitals, HALO, cells), jnp.float32)
        local_out[start : start + HALO] = jnp.zeros((HALO, cells), jnp.float32)
        trial_out[:, start : start + HALO] = jnp.zeros((half, HALO, cells), jnp.float32)

    @pl.when(jnp.logical_not(has_up))
    def _():
        clear(0)

    @pl.when(jnp.logical_not(has_down))
    def _():
        clear(last)

    def owner_of(line):
        return owner_ref[(ring.side * half + line // split) // kinds]

    sent = []
    for step, copy in copies:
        line = ring.peer(step)
        copy.wait_recv()
        mine = piece(pot_ref.at[ring.side], ring.lines, line, 0, rows)[...]
        value = jnp.where(owner_of(line) == ring.partner, crossed[line], mine)
        if step == 0:
            gathered[ring.line] = value
        else:
            merged[step] = value
            out = send(
                merged.at[step], gathered.at[ring.line],
                scatter_sems.at[0, line], scatter_sems.at[1, ring.line], ring.at_line(line),
            )
            out.start()
            sent.append(out)
    for step in range(1, ring.lines):
        line = ring.peer(step)
        send(
            merged.at[step], gathered.at[line],
            scatter_sems.at[0, line], scatter_sems.at[1, line], ring.at_line(line),
        ).wait_recv()
    piece(trial_out, ring.lines, ring.line, HALO, rows)[...] = gathered[owner_of(ring.line) // PAIR]

    def halo_up(index):
        return send(
            piece(trial_out, ring.lines, index, HALO, HALO),
            piece(trial_out, ring.lines, index, last, HALO),
            halo_sems.at[0, 0, index], halo_sems.at[1, 0, index], ring.up(),
        )

    def halo_down(index):
        return send(
            piece(trial_out, ring.lines, index, rows, HALO),
            piece(trial_out, ring.lines, index, 0, HALO),
            halo_sems.at[0, 1, index], halo_sems.at[1, 1, index], ring.down(),
        )

    def arrived(index):
        @pl.when(has_up)
        def _():
            halo_up(index).start()

        @pl.when(has_down)
        def _():
            halo_down(index).start()

        return []

    def arrived_first(index):
        arrived(index)
        center.wait_recv()

        @pl.when(has_up)
        def _():
            edge_up(ring.up())[2].start()

        @pl.when(has_down)
        def _():
            edge_down(ring.down())[2].start()

        return []

    calls = [arrived_first] + [arrived] * (ring.lines - 1)
    sent += line_gather(
        ring, trial_out, HALO, rows, line_sems, lambda index: calls.pop(0)(index)
    )

    @pl.when(has_up)
    def _():
        for copy in edge_up(ring.up()):
            copy.wait_send()
        for copy in edge_down(ring.up()):
            copy.wait_recv()
        for index in range(ring.lines):
            halo_up(index).wait_send()
            halo_down(index).wait_recv()

    @pl.when(has_down)
    def _():
        for copy in edge_down(ring.down()):
            copy.wait_send()
        for copy in edge_up(ring.down()):
            copy.wait_recv()
        for index in range(ring.lines):
            halo_down(index).wait_send()
            halo_up(index).wait_recv()

    pack.wait_recv()
    for copy in [copy for step, copy in copies] + sent + [center, pack]:
        copy.wait_send()


def total_kernel(count, grids, part_ref, out_ref, gathered, scatter_sems, line_sems, side_sems):
    ring = Ring(count, grids)
    rows = part_ref.shape[1]
    enter(ring, False)
    sent = []
    for step in range(1, ring.lines):
        line = ring.peer(step)
        out = send(
            piece(part_ref, ring.lines, line, 0, rows), gathered.at[ring.line],
            scatter_sems.at[0, line], scatter_sems.at[1, ring.line], ring.at_line(line),
        )
        out.start()
        sent.append(out)
    own = piece(part_ref, ring.lines, ring.line, 0, rows)
    total = own[...]
    for step in range(1, ring.lines):
        line = ring.peer(ring.lines - step)
        send(
            own, gathered.at[line],
            scatter_sems.at[0, line], scatter_sems.at[1, line], ring.at_line(line),
        ).wait_recv()
        total = total + gathered[line]
    mine, other = out_ref.at[ring.side], out_ref.at[1 - ring.side]
    piece(mine, ring.lines, ring.line, 0, rows)[...] = total

    def arrived(line):
        part = piece(mine, ring.lines, line, 0, rows)
        out = send(part, part, side_sems.at[0, line], side_sems.at[1, line], ring.across())
        out.start()
        return [out]

    sent += line_gather(ring, mine, 0, rows, line_sems, arrived)
    for step in range(ring.lines):
        line = ring.peer(ring.lines - step)
        part = piece(other, ring.lines, line, 0, rows)
        send(part, part, side_sems.at[0, line], side_sems.at[1, line], ring.across()).wait_recv()
    for copy in sent:
        copy.wait_send()


def band_matrix(depth, width):
    k = lax.broadcasted_iota(jnp.int32, (depth, width), 0)
    n = lax.broadcasted_iota(jnp.int32, (depth, width), 1) + width // 2
    far_y, far_z = jnp.abs(k // NZ - n // NZ), jnp.abs(k % NZ - n % NZ)
    near = ((far_y == 1) & (far_z == 0)) | ((far_y == 0) & (far_z == 1))
    far = ((far_y == 2) & (far_z == 0)) | ((far_y == 0) & (far_z == 2))
    return jnp.where(near, 16.0, jnp.where(far, -1.0, 0.0)).astype(jnp.bfloat16)


WIDTH = 256


def sweep_kernel(
    grids, pack_ref, trial_ref, orb_ref, local_ref, out_ref,
    trials, first, scale, now_a, now_b, hi_a, hi_b, lo_a, lo_b, product, density, band, inverse,
    weighted,
):
    n = pl.program_id(0)
    half, planes, cells = trial_ref.shape
    orbitals = orb_ref.shape[1]
    batch = PAIR * half
    rows = planes - 2 * HALO

    @pl.when(n == 0)
    def _():
        band[...] = band_matrix(2 * WIDTH, WIDTH)
        density[...] = jnp.zeros_like(density)
        for x in range(planes):
            trials[x] = jnp.concatenate([trial_ref[:, x, :]] * PAIR, axis=0)

    place = lax.axis_index("grid") * rows - HALO
    where = lax.broadcasted_iota(jnp.int32, (planes, cells), 0) + place
    inside = (where >= 0) & (where < rows * grids)
    for k in range(PAIR):
        diagonal = KINETIC_DIAG + (local_ref[...] + pack_ref[k, pl.ds(n, 1), :])
        inverse[k] = jnp.where(inside, 1.0 / diagonal, 0.0)

    lower = lax.broadcasted_iota(jnp.int32, (batch, cells), 0) < half

    def both(a, b):
        return jnp.where(
            lower, jnp.broadcast_to(a, (batch, cells)), jnp.broadcast_to(b, (batch, cells))
        )

    def split(value):
        high = value.astype(jnp.bfloat16)
        return high, (value - high.astype(jnp.float32)).astype(jnp.bfloat16)

    weight = both(pack_ref[0, pl.ds(orbitals + n, 1), :], pack_ref[1, pl.ds(orbitals + n, 1), :])
    for x in range(0, planes, 2):
        values = []
        for p in (x, x + 1):
            inv = both(inverse[0, pl.ds(p, 1), :], inverse[1, pl.ds(p, 1), :])
            orb = both(orb_ref[0, n, pl.ds(p, 1), :], orb_ref[1, n, pl.ds(p, 1), :])
            scale[p] = inv * (1.0 / 24.0)
            value = -(trials[p] * orb) * inv
            first[p] = value
            values.append(value)
            if HALO <= p < HALO + rows:
                weighted[p - HALO] = weight * orb
        high, low = split(jnp.concatenate(values, axis=0))
        hi_a[x * batch : (x + 2) * batch] = high
        lo_a[x * batch : (x + 2) * batch] = low

    current = first
    buffers = ((now_a, hi_a, lo_a), (now_b, hi_b, lo_b))
    for repeat in range(ITERS):
        hi_in, lo_in = buffers[repeat % 2][1:]
        target, hi_out, lo_out = buffers[(repeat + 1) % 2]
        margin = REACH * (repeat + 1)
        extent = planes - 2 * margin
        for left in range(0, cells, WIDTH):
            a = max(0, left - WIDTH // 2)
            b = min(cells, left + WIDTH + WIDTH // 2)
            k = a - (left - WIDTH // 2)
            weights = band[k : k + b - a, :]
            span = slice(margin * batch, (margin + extent) * batch)
            product[0 : extent * batch] = jnp.dot(
                hi_in[span, a:b], weights, preferred_element_type=jnp.float32
            ) + jnp.dot(lo_in[span, a:b], weights, preferred_element_type=jnp.float32)
            lanes = slice(left, left + WIDTH)
            for x in range(margin, margin + extent, 2):
                values = []
                for p in (x, x + 1):
                    near = current[p - 1, :, lanes] + current[p + 1, :, lanes]
                    far = current[p - 2, :, lanes] + current[p + 2, :, lanes]
                    spot = (p - margin) * batch
                    moved = product[spot : spot + batch] + (16.0 * near - far)
                    value = first[p, :, lanes] + scale[p, :, lanes] * moved
                    if repeat == ITERS - 1:
                        density[p - margin, :, lanes] += weighted[p - margin, :, lanes] * value
                    else:
                        target[p, :, lanes] = value
                        values.append(value)
                if values:
                    high, low = split(jnp.concatenate(values, axis=0))
                    hi_out[x * batch : (x + 2) * batch, lanes] = high
                    lo_out[x * batch : (x + 2) * batch, lanes] = low
        current = target

    @pl.when(n == pl.num_programs(0) - 1)
    def _():
        for x in range(rows):
            out_ref[:, x, :] = density[x, 0:half] + density[x, half:batch]


def shards(count, grids, potentials, orbitals, local_pot, shifts, occupation, owner):
    _, blocks, kinds, rows, cells = potentials.shape
    batch = blocks * kinds
    half = batch // PAIR
    orbital_count = orbitals.shape[0]
    lines = count // PAIR
    planes = rows + 2 * HALO
    stored = potentials.reshape(PAIR, half, rows, cells)
    vmem = pl.BlockSpec(memory_space=pltpu.VMEM)
    smem = pl.BlockSpec(memory_space=pltpu.SMEM)
    f32 = jnp.float32
    dma = pltpu.SemaphoreType.DMA
    slots = pltpu.VMEM((lines, rows, cells * half // lines), f32)
    trials, orbs, local, pack = pl.pallas_call(
        functools.partial(spread_kernel, count, grids, kinds),
        out_shape=[
            jax.ShapeDtypeStruct((half, planes, cells), f32),
            jax.ShapeDtypeStruct((PAIR, orbital_count, planes, cells), f32),
            jax.ShapeDtypeStruct((planes, cells), f32),
            jax.ShapeDtypeStruct((PAIR, 2 * orbital_count, cells), f32),
        ],
        in_specs=[smem, smem, smem, vmem, vmem, vmem],
        out_specs=[vmem] * 4,
        scratch_shapes=[
            slots, slots, slots,
            dma((2, lines)), dma((2, lines)), dma((2, lines)),
            dma((2, 2, lines)), dma((2, 6)), dma((2, 2)),
        ],
        compiler_params=pltpu.CompilerParams(collective_id=0, has_side_effects=True),
        name="spread",
    )(owner, shifts, occupation, stored, orbitals, local_pot)

    big = pltpu.VMEM((planes, batch, cells), f32)
    packed = pltpu.VMEM((planes * batch, cells), jnp.bfloat16)
    partial = pl.pallas_call(
        functools.partial(sweep_kernel, grids),
        out_shape=jax.ShapeDtypeStruct((half, rows, cells), f32),
        grid=(orbital_count,),
        in_specs=[vmem] * 4,
        out_specs=vmem,
        scratch_shapes=[big, big, big, big, big, packed, packed, packed, packed]
        + [
            pltpu.VMEM((planes * batch, WIDTH), f32),
            pltpu.VMEM((rows, batch, cells), f32),
            pltpu.VMEM((2 * WIDTH, WIDTH), jnp.bfloat16),
            pltpu.VMEM((PAIR, planes, cells), f32),
            pltpu.VMEM((rows, batch, cells), f32),
        ],
        compiler_params=pltpu.CompilerParams(dimension_semantics=("arbitrary",)),
        name="sweeps",
    )(pack, trials, orbs, local)

    totals = pl.pallas_call(
        functools.partial(total_kernel, count, grids),
        out_shape=jax.ShapeDtypeStruct((PAIR, half, rows, cells), f32),
        in_specs=[vmem],
        out_specs=vmem,
        scratch_shapes=[slots, dma((2, lines)), dma((2, lines)), dma((2, lines))],
        compiler_params=pltpu.CompilerParams(collective_id=1, has_side_effects=True),
        name="total",
    )(partial)
    owned = (owner == lax.axis_index("orb"))[:, None, None, None]
    return jnp.where(owned, totals.reshape(blocks, kinds, rows, cells), 0.0)[None]


def solution(mesh):
    in_specs = (
        P("orb", None, None, "grid", None),
        P("orb", "grid", None),
        P("grid", None),
        P("orb"),
        P("orb"),
        P(),
    )
    out_specs = P("orb", None, None, "grid", None)
    body = functools.partial(shards, mesh.shape["orb"], mesh.shape["grid"])
    return jax.shard_map(body, mesh=mesh, in_specs=in_specs, out_specs=out_specs, check_vma=False)
```

time: 70.5 us -> 63.6 us (0.902)
  Pallas kernels: 67.6 us -> 60.7 us
    pallas_call x1, Pallas kernels: 26.9 us -> 23.1 us  [shards(): pl.pallas_call(functools.partial(total_kernel, count, grids), out_shape=j...]
    pallas_call x1, Pallas kernels: 29.1 us -> 25.4 us  [shards(): pl.pallas_call(functools.partial(spread_kernel, count, grids, kinds), out...]
    broadcast_in_dim x0 -> x1, other arithmetic: none -> 1.95 us  [shards(): jnp.where(owned, totals.reshape(blocks, kinds, rows, cells), 0.0)[None]]
    select_n x1 -> x0, other arithmetic: 1.95 us -> none  [shards(): jnp.where(owned, totals.reshape(blocks, kinds, rows, cells), 0.0)[None]]
where the time goes in v2:
time: 63.6 us; the launch traced here: 63.3 us
  Pallas kernels  60.7 us (95%)
  other arithmetic  1.96 us (3%)
  local copies, waits for them, and re-layouts  0.65 us (1%)
    pallas_call x1, Pallas kernels, shards(): pl.pallas_call(functools.partial(spread_kernel, count, grids, kinds), out...  25.4 us
    pallas_call x1, Pallas kernels, shards(): pl.pallas_call(functools.partial(total_kernel, count, grids), out_shape=j...  23.1 us
    pallas_call x1, Pallas kernels, shards(): pl.pallas_call(functools.partial(sweep_kernel, grids), out_shape=jax.Shap...  12.2 us
    broadcast_in_dim x1, other arithmetic, shards(): jnp.where(owned, totals.reshape(blocks, kinds, rows, cells), 0.0)[None]  1.95 us

profile of v2, /device:TPU:0, one launch (start us, length us, event | category | flops | bytes accessed | tf_op | source)
XLA Modules:
  0.0 63.3 jit_solution(12541577215468788608)
XLA Ops:
  0.0 25.4 %spread.1 = (f32[4,32,1024]{2,1,0:T(8,128)}, f32[2,4,32,1024]{3,2,1,0:T(8,128)}, f32[32,1024]{1,0:T(8,128)}, f32[2,8,1024]{2,1,0:T(8,128)}) custom-call(s32[2]{0:T(128)} %owner_ref.1, f32[4]{0:T(128)} %shift_ref.1, s32[4]{0:T(128)} %weight_ref.1, f32[2,4,16,1024]{3,2,1,0:T(8,128)} %bitcast.3, f32[4,16,1024]{2,1,0:T(8,128)} %orb_ref.1, f32[16,1024]{1,0:T(8,128)} %local_ref.1), custom_call_target="tpu_custom_call" | custom-call | tf_op jit(solution)/shard_map/spread/pallas_call | solution.py:437
  25.4 12.2 %sweeps.1.part_ref = f32[4,16,1024]{2,1,0:T(8,128)} custom-call(f32[2,8,1024]{2,1,0:T(8,128)} %get-tuple-element.9.pack_ref, f32[4,32,1024]{2,1,0:T(8,128)} %get-tuple-element.10.trial_ref, f32[2,4,32,1024]{3,2,1,0:T(8,128)} %get-tuple-element.11.orb_ref, f32[32,1024]{1,0:T(8,128)} %get-tuple-element.12.local_ref), custom_call_target="tpu_custom_call" | custom-call | tf_op jit(solution)/shard_map/sweeps/pallas_call | solution.py:458
  37.6 23.1 %total.1 = f32[2,4,16,1024]{3,2,1,0:T(8,128)} custom-call(f32[4,16,1024]{2,1,0:T(8,128)} %sweeps.1.part_ref), custom_call_target="tpu_custom_call" | custom-call | tf_op jit(solution)/shard_map/total/pallas_call | solution.py:476
  60.7 0.0 copy-start
  60.7 0.6 %copy-done = s32[2]{0:T(128)S(1)} copy-done((s32[2]{0:T(128)S(1)}, s32[2]{0:T(128)}, u32[]{:S(2)}) %copy-start) | copy-done | bytes 32
  61.4 2.0 %select_bitcast_fusion = f32[1,2,4,16,1024]{4,3,2,1,0:T(8,128)} fusion(f32[2,4,16,1024]{3,2,1,0:T(8,128)} %total.1, pred[2]{0:T(512)(128)(4,1)S(1)} %broadcast_compare_fusion), kind=kLoop, calls=%fused_computation | loop fusion | flops 131072 | bytes 1048578 | tf_op jit(solution)/shard_map/broadcast_in_dim | solution.py:486
  (1 shorter events, 0.0 us)
Async XLA Ops:
  60.7 0.7 %copy-start = (s32[2]{0:T(128)S(1)}, s32[2]{0:T(128)}, u32[]{:S(2)}) copy-start(s32[2]{0:T(128)} %owner_ref.1) | copy-start | bytes 28

commit v3 on v2

v3 whole, which is shorter than its diff:
```python
import functools

import jax
import jax.numpy as jnp
from jax import lax
from jax.experimental import pallas as pl
from jax.experimental.pallas import tpu as pltpu
from jax.sharding import PartitionSpec as P

NZ = 32
ITERS = 4
REACH = 2
HALO = REACH * ITERS
KINETIC_DIAG = 3.75
PAIR = 2
MESH = pl.DeviceIdType.MESH


class Ring:
    def __init__(self, count, grids):
        self.count, self.lines, self.grids = count, count // PAIR, grids
        self.me = lax.axis_index("orb")
        self.row = lax.axis_index("grid")
        self.line, self.side = self.me // PAIR, self.me % PAIR
        self.partner = self.line * PAIR + (1 - self.side)

    def at_line(self, line):
        return {"orb": line * PAIR + self.side, "grid": self.row}

    def across(self):
        return {"orb": self.partner, "grid": self.row}

    def up(self):
        return {"orb": self.me, "grid": self.row - 1}

    def down(self):
        return {"orb": self.me, "grid": self.row + 1}


def enter(ring, with_grid):
    barrier = pltpu.get_barrier_semaphore()
    top = ring.lines - 1

    def greet(target):
        pl.semaphore_signal(barrier, inc=1, device_id=target, device_id_type=MESH)

    greet(ring.across())

    @pl.when(ring.line > 0)
    def _():
        greet(ring.at_line(ring.line - 1))

    @pl.when(ring.line < top)
    def _():
        greet(ring.at_line(ring.line + 1))

    peers = 1 + (ring.line + top) // ring.lines + (2 * top - ring.line) // ring.lines
    if with_grid:

        @pl.when(ring.row > 0)
        def _():
            greet(ring.up())

        @pl.when(ring.row < ring.grids - 1)
        def _():
            greet(ring.down())

        last = ring.grids - 1
        peers = peers + (ring.row + last) // ring.grids + (2 * last - ring.row) // ring.grids
    pl.semaphore_wait(barrier, peers)


def send(src, dst, send_sem, recv_sem, target):
    return pltpu.make_async_remote_copy(
        src_ref=src, dst_ref=dst, send_sem=send_sem, recv_sem=recv_sem,
        device_id=target, device_id_type=MESH,
    )


LAG = 2


class Waves:
    def __init__(self, ring, chunks, buffers, sems):
        self.ring, self.chunks, self.sems = ring, chunks, sems
        self.from_left, self.from_right, self.to_right, self.to_left = buffers
        self.has_left, self.has_right = ring.line > 0, ring.line < ring.lines - 1

    def right(self, q, target):
        sems = self.sems
        return send(self.to_right.at[q], self.from_left.at[q], sems.at[0, q], sems.at[1, q], target)

    def left(self, q, target):
        sems = self.sems
        return send(self.to_left.at[q], self.from_right.at[q], sems.at[2, q], sems.at[3, q], target)

    def clear(self):
        @pl.when(jnp.logical_not(self.has_left))
        def _():
            self.from_left[...] = jnp.zeros_like(self.from_left)

        @pl.when(jnp.logical_not(self.has_right))
        def _():
            self.from_right[...] = jnp.zeros_like(self.from_right)

    def run(self, prepare, onward, finish):
        ring, line, top = self.ring, self.ring.line, self.ring.lines - 1
        beyond = (2 * line) // ring.lines
        late = beyond * line + (1 - beyond) * (top - line)

        def step(s, carry):
            def event(offset, act):
                q = s - offset

                @pl.when((q >= 0) & (q < self.chunks))
                def _():
                    act(q)

            def rightward(q):
                @pl.when(self.has_left)
                def _():
                    self.right(q, ring.across()).wait_recv()

                @pl.when(self.has_right)
                def _():
                    self.to_right[q] = onward(q, self.from_left[q])
                    self.right(q, ring.at_line(line + 1)).start()

            def leftward(q):
                @pl.when(self.has_right)
                def _():
                    self.left(q, ring.across()).wait_recv()

                @pl.when(self.has_left)
                def _():
                    self.to_left[q] = onward(q, self.from_right[q])
                    self.left(q, ring.at_line(line - 1)).start()

            event(0, prepare)
            event(line * LAG, rightward)
            event((top - line) * LAG, leftward)
            event(late * LAG, finish)
            return carry

        lax.fori_loop(0, self.chunks + top * LAG, step, 0)

    def drain(self):
        @pl.when(self.has_right)
        def _():
            for q in range(self.chunks):
                self.right(q, self.ring.across()).wait_send()

        @pl.when(self.has_left)
        def _():
            for q in range(self.chunks):
                self.left(q, self.ring.across()).wait_send()


def chunk_of(ref, q, per, start=0):
    return ref.at[q // per, pl.ds(pl.multiple_of(start + (q % per) * HALO, HALO), HALO)]


def spread_kernel(
    count, grids, kinds, owner_ref, shift_ref, weight_ref, pot_ref, orb_ref, local_ref,
    trial_out, orb_out, local_out, pack_out,
    crossed, merged, from_left, from_right, to_right, to_left,
    cross_sems, wave_sems, halo_sems, edge_sems, pair_sems,
):
    ring = Ring(count, grids)
    orbitals, rows, cells = orb_ref.shape
    half = pot_ref.shape[1]
    per = rows // HALO
    chunks = half * per
    last = HALO + rows
    has_up, has_down = ring.row > 0, ring.row < grids - 1
    waves = Waves(ring, chunks, (from_left, from_right, to_right, to_left), wave_sems)
    for n in range(orbitals):
        pack_out[0, n] = jnp.full((cells,), shift_ref[n], jnp.float32)
        pack_out[0, orbitals + n] = jnp.full((cells,), weight_ref[n].astype(jnp.float32), jnp.float32)
    enter(ring, True)

    def cross(q):
        return send(
            chunk_of(pot_ref.at[1 - ring.side], q, per), crossed.at[q],
            cross_sems.at[0, q], cross_sems.at[1, q], ring.across(),
        )

    for q in range(chunks):
        cross(q).start()
    center = send(
        orb_ref, orb_out.at[1, :, pl.ds(HALO, rows)],
        pair_sems.at[0, 0], pair_sems.at[1, 0], ring.across(),
    )
    center.start()
    pack = send(
        pack_out.at[0], pack_out.at[1], pair_sems.at[0, 1], pair_sems.at[1, 1], ring.across()
    )
    pack.start()

    def edge_up(k, target):
        src, dst = [
            (orb_ref.at[:, pl.ds(0, HALO)], orb_out.at[0, :, pl.ds(last, HALO)]),
            (local_ref.at[pl.ds(0, HALO)], local_out.at[pl.ds(last, HALO)]),
            (orb_out.at[1, :, pl.ds(HALO, HALO)], orb_out.at[1, :, pl.ds(last, HALO)]),
        ][k]
        return send(src, dst, edge_sems.at[0, k], edge_sems.at[1, k], target)

    def edge_down(k, target):
        src, dst = [
            (orb_ref.at[:, pl.ds(rows - HALO, HALO)], orb_out.at[0, :, pl.ds(0, HALO)]),
            (local_ref.at[pl.ds(rows - HALO, HALO)], local_out.at[pl.ds(0, HALO)]),
            (orb_out.at[1, :, pl.ds(rows, HALO)], orb_out.at[1, :, pl.ds(0, HALO)]),
        ][k]
        return send(src, dst, edge_sems.at[0, 3 + k], edge_sems.at[1, 3 + k], target)

    @pl.when(has_up)
    def _():
        for k in range(2):
            edge_up(k, ring.up()).start()

    @pl.when(has_down)
    def _():
        for k in range(2):
            edge_down(k, ring.down()).start()

    waves.clear()
    orb_out[0, :, HALO:last] = orb_ref[...]
    local_out[HALO:last] = local_ref[...]

    def clear(start):
        orb_out[:, :, start : start + HALO] = jnp.zeros((2, orbitals, HALO, cells), jnp.float32)
        local_out[start : start + HALO] = jnp.zeros((HALO, cells), jnp.float32)
        trial_out[:, start : start + HALO] = jnp.zeros((half, HALO, cells), jnp.float32)

    @pl.when(jnp.logical_not(has_up))
    def _():
        clear(0)

    @pl.when(jnp.logical_not(has_down))
    def _():
        clear(last)

    def owner_of(q):
        return owner_ref[(ring.side * half + q // per) // kinds]

    def prepare(q):
        cross(q).wait_recv()
        mine = chunk_of(pot_ref.at[ring.side], q, per)[...]
        merged[q] = jnp.where(owner_of(q) == ring.partner, crossed[q], mine)

    def onward(q, came):
        return jnp.where(owner_of(q) // PAIR == ring.line, merged[q], came)

    def halo_up(t, target):
        return send(
            trial_out.at[t, pl.ds(HALO, HALO)], trial_out.at[t, pl.ds(last, HALO)],
            halo_sems.at[0, 0, t], halo_sems.at[1, 0, t], target,
        )

    def halo_down(t, target):
        return send(
            trial_out.at[t, pl.ds(rows, HALO)], trial_out.at[t, pl.ds(0, HALO)],
            halo_sems.at[0, 1, t], halo_sems.at[1, 1, t], target,
        )

    def finish(q):
        place = owner_of(q) // PAIR
        other = jnp.where(place < ring.line, waves.from_left[q], waves.from_right[q])
        value = jnp.where(place == ring.line, merged[q], other)
        chunk_of(trial_out, q, per, HALO)[...] = value

        @pl.when(has_up & (q % per == 0))
        def _():
            halo_up(q // per, ring.up()).start()

        @pl.when(has_down & (q % per == per - 1))
        def _():
            halo_down(q // per, ring.down()).start()

    waves.run(prepare, onward, finish)
    center.wait_recv()

    @pl.when(has_up)
    def _():
        edge_up(2, ring.up()).start()

    @pl.when(has_down)
    def _():
        edge_down(2, ring.down()).start()

    @pl.when(has_up)
    def _():
        for k in range(3):
            edge_up(k, ring.across()).wait_send()
            edge_down(k, ring.across()).wait_recv()
        for t in range(half):
            halo_up(t, ring.across()).wait_send()
            halo_down(t, ring.across()).wait_recv()

    @pl.when(has_down)
    def _():
        for k in range(3):
            edge_down(k, ring.across()).wait_send()
            edge_up(k, ring.across()).wait_recv()
        for t in range(half):
            halo_down(t, ring.across()).wait_send()
            halo_up(t, ring.across()).wait_recv()

    pack.wait()
    center.wait_send()
    for q in range(chunks):
        cross(q).wait_send()
    waves.drain()


def total_kernel(
    count, grids, part_ref, out_ref, from_left, from_right, to_right, to_left, wave_sems, side_sems
):
    ring = Ring(count, grids)
    half, rows, _ = part_ref.shape
    per = rows // HALO
    chunks = half * per
    waves = Waves(ring, chunks, (from_left, from_right, to_right, to_left), wave_sems)
    waves.clear()
    enter(ring, False)
    mine, other = out_ref.at[ring.side], out_ref.at[1 - ring.side]

    def across(view, q):
        part = chunk_of(view, q, per)
        return send(part, part, side_sems.at[0, q], side_sems.at[1, q], ring.across())

    def onward(q, came):
        return came + chunk_of(part_ref, q, per)[...]

    def finish(q):
        total = waves.from_left[q] + chunk_of(part_ref, q, per)[...] + waves.from_right[q]
        chunk_of(mine, q, per)[...] = total
        across(mine, q).start()

    waves.run(lambda q: None, onward, finish)
    for q in range(chunks):
        across(other, q).wait_recv()
        across(mine, q).wait_send()
    waves.drain()


def band_matrix(depth, width):
    k = lax.broadcasted_iota(jnp.int32, (depth, width), 0)
    n = lax.broadcasted_iota(jnp.int32, (depth, width), 1) + width // 2
    far_y, far_z = jnp.abs(k // NZ - n // NZ), jnp.abs(k % NZ - n % NZ)
    near = ((far_y == 1) & (far_z == 0)) | ((far_y == 0) & (far_z == 1))
    far = ((far_y == 2) & (far_z == 0)) | ((far_y == 0) & (far_z == 2))
    return jnp.where(near, 16.0, jnp.where(far, -1.0, 0.0)).astype(jnp.bfloat16)


WIDTH = 256


def sweep_kernel(
    grids, pack_ref, trial_ref, orb_ref, local_ref, out_ref,
    trials, first, scale, now_a, now_b, hi_a, hi_b, lo_a, lo_b, product, density, band, inverse,
    weighted,
):
    n = pl.program_id(0)
    half, planes, cells = trial_ref.shape
    orbitals = orb_ref.shape[1]
    batch = PAIR * half
    rows = planes - 2 * HALO

    @pl.when(n == 0)
    def _():
        band[...] = band_matrix(2 * WIDTH, WIDTH)
        density[...] = jnp.zeros_like(density)
        for x in range(planes):
            trials[x] = jnp.concatenate([trial_ref[:, x, :]] * PAIR, axis=0)

    place = lax.axis_index("grid") * rows - HALO
    where = lax.broadcasted_iota(jnp.int32, (planes, cells), 0) + place
    inside = (where >= 0) & (where < rows * grids)
    for k in range(PAIR):
        diagonal = KINETIC_DIAG + (local_ref[...] + pack_ref[k, pl.ds(n, 1), :])
        inverse[k] = jnp.where(inside, 1.0 / diagonal, 0.0)

    lower = lax.broadcasted_iota(jnp.int32, (batch, cells), 0) < half

    def both(a, b):
        return jnp.where(
            lower, jnp.broadcast_to(a, (batch, cells)), jnp.broadcast_to(b, (batch, cells))
        )

    def split(value):
        high = value.astype(jnp.bfloat16)
        return high, (value - high.astype(jnp.float32)).astype(jnp.bfloat16)

    weight = both(pack_ref[0, pl.ds(orbitals + n, 1), :], pack_ref[1, pl.ds(orbitals + n, 1), :])
    for x in range(0, planes, 2):
        values = []
        for p in (x, x + 1):
            inv = both(inverse[0, pl.ds(p, 1), :], inverse[1, pl.ds(p, 1), :])
            orb = both(orb_ref[0, n, pl.ds(p, 1), :], orb_ref[1, n, pl.ds(p, 1), :])
            scale[p] = inv * (1.0 / 24.0)
            value = -(trials[p] * orb) * inv
            first[p] = value
            values.append(value)
            if HALO <= p < HALO + rows:
                weighted[p - HALO] = weight * orb
        high, low = split(jnp.concatenate(values, axis=0))
        hi_a[x * batch : (x + 2) * batch] = high
        lo_a[x * batch : (x + 2) * batch] = low

    current = first
    buffers = ((now_a, hi_a, lo_a), (now_b, hi_b, lo_b))
    for repeat in range(ITERS):
        hi_in, lo_in = buffers[repeat % 2][1:]
        target, hi_out, lo_out = buffers[(repeat + 1) % 2]
        margin = REACH * (repeat + 1)
        extent = planes - 2 * margin
        for left in range(0, cells, WIDTH):
            a = max(0, left - WIDTH // 2)
            b = min(cells, left + WIDTH + WIDTH // 2)
            k = a - (left - WIDTH // 2)
            weights = band[k : k + b - a, :]
            span = slice(margin * batch, (margin + extent) * batch)
            product[0 : extent * batch] = jnp.dot(
                hi_in[span, a:b], weights, preferred_element_type=jnp.float32
            ) + jnp.dot(lo_in[span, a:b], weights, preferred_element_type=jnp.float32)
            lanes = slice(left, left + WIDTH)
            for x in range(margin, margin + extent, 2):
                values = []
                for p in (x, x + 1):
                    near = current[p - 1, :, lanes] + current[p + 1, :, lanes]
                    far = current[p - 2, :, lanes] + current[p + 2, :, lanes]
                    spot = (p - margin) * batch
                    moved = product[spot : spot + batch] + (16.0 * near - far)
                    value = first[p, :, lanes] + scale[p, :, lanes] * moved
                    if repeat == ITERS - 1:
                        density[p - margin, :, lanes] += weighted[p - margin, :, lanes] * value
                    else:
                        target[p, :, lanes] = value
                        values.append(value)
                if values:
                    high, low = split(jnp.concatenate(values, axis=0))
                    hi_out[x * batch : (x + 2) * batch, lanes] = high
                    lo_out[x * batch : (x + 2) * batch, lanes] = low
        current = target

    @pl.when(n == pl.num_programs(0) - 1)
    def _():
        for x in range(rows):
            out_ref[:, x, :] = density[x, 0:half] + density[x, half:batch]


def shards(count, grids, potentials, orbitals, local_pot, shifts, occupation, owner):
    _, blocks, kinds, rows, cells = potentials.shape
    batch = blocks * kinds
    half = batch // PAIR
    orbital_count = orbitals.shape[0]
    planes = rows + 2 * HALO
    stored = potentials.reshape(PAIR, half, rows, cells)
    vmem = pl.BlockSpec(memory_space=pltpu.VMEM)
    smem = pl.BlockSpec(memory_space=pltpu.SMEM)
    f32 = jnp.float32
    dma = pltpu.SemaphoreType.DMA
    chunks = half * (rows // HALO)
    slots = pltpu.VMEM((chunks, HALO, cells), f32)
    trials, orbs, local, pack = pl.pallas_call(
        functools.partial(spread_kernel, count, grids, kinds),
        out_shape=[
            jax.ShapeDtypeStruct((half, planes, cells), f32),
            jax.ShapeDtypeStruct((PAIR, orbital_count, planes, cells), f32),
            jax.ShapeDtypeStruct((planes, cells), f32),
            jax.ShapeDtypeStruct((PAIR, 2 * orbital_count, cells), f32),
        ],
        in_specs=[smem, smem, smem, vmem, vmem, vmem],
        out_specs=[vmem] * 4,
        scratch_shapes=[
            slots, slots, slots, slots, slots, slots,
            dma((2, chunks)), dma((4, chunks)), dma((2, 2, half)), dma((2, 6)), dma((2, 2)),
        ],
        compiler_params=pltpu.CompilerParams(collective_id=0, has_side_effects=True),
        name="spread",
    )(owner, shifts, occupation, stored, orbitals, local_pot)

    big = pltpu.VMEM((planes, batch, cells), f32)
    packed = pltpu.VMEM((planes * batch, cells), jnp.bfloat16)
    partial = pl.pallas_call(
        functools.partial(sweep_kernel, grids),
        out_shape=jax.ShapeDtypeStruct((half, rows, cells), f32),
        grid=(orbital_count,),
        in_specs=[vmem] * 4,
        out_specs=vmem,
        scratch_shapes=[big, big, big, big, big, packed, packed, packed, packed]
        + [
            pltpu.VMEM((planes * batch, WIDTH), f32),
            pltpu.VMEM((rows, batch, cells), f32),
            pltpu.VMEM((2 * WIDTH, WIDTH), jnp.bfloat16),
            pltpu.VMEM((PAIR, planes, cells), f32),
            pltpu.VMEM((rows, batch, cells), f32),
        ],
        compiler_params=pltpu.CompilerParams(dimension_semantics=("arbitrary",)),
        name="sweeps",
    )(pack, trials, orbs, local)

    totals = pl.pallas_call(
        functools.partial(total_kernel, count, grids),
        out_shape=jax.ShapeDtypeStruct((PAIR, half, rows, cells), f32),
        in_specs=[vmem],
        out_specs=vmem,
        scratch_shapes=[slots, slots, slots, slots, dma((4, chunks)), dma((2, chunks))],
        compiler_params=pltpu.CompilerParams(collective_id=1, has_side_effects=True),
        name="total",
    )(partial)
    owned = (owner == lax.axis_index("orb"))[:, None, None, None]
    return jnp.where(owned, totals.reshape(blocks, kinds, rows, cells), 0.0)[None]


def solution(mesh):
    in_specs = (
        P("orb", None, None, "grid", None),
        P("orb", "grid", None),
        P("grid", None),
        P("orb"),
        P("orb"),
        P(),
    )
    out_specs = P("orb", None, None, "grid", None)
    body = functools.partial(shards, mesh.shape["orb"], mesh.shape["grid"])
    return jax.shard_map(body, mesh=mesh, in_specs=in_specs, out_specs=out_specs, check_vma=False)
```

time: 63.6 us -> 69.5 us (1.093); the launches traced: 63.3 us -> 68.4 us
  Pallas kernels: 60.7 us -> 65.8 us
    pallas_call x1, Pallas kernels: 25.4 us -> 29.2 us  [shards(): pl.pallas_call(functools.partial(spread_kernel, count, grids, kinds), out...]
    pallas_call x1, Pallas kernels: 23.1 us -> 24.4 us  [shards(): pl.pallas_call(functools.partial(total_kernel, count, grids), out_shape=j...]
where the time goes in v3:
time: 69.5 us; the launch traced here: 68.4 us
  Pallas kernels  65.8 us (95%)
  other arithmetic  1.96 us (3%)
    pallas_call x1, Pallas kernels, shards(): pl.pallas_call(functools.partial(spread_kernel, count, grids, kinds), out...  29.2 us
    pallas_call x1, Pallas kernels, shards(): pl.pallas_call(functools.partial(total_kernel, count, grids), out_shape=j...  24.4 us
    pallas_call x1, Pallas kernels, shards(): pl.pallas_call(functools.partial(sweep_kernel, grids), out_shape=jax.Shap...  12.2 us
    broadcast_in_dim x1, other arithmetic, shards(): jnp.where(owned, totals.reshape(blocks, kinds, rows, cells), 0.0)[None]  1.95 us

profile of v3, /device:TPU:0, one launch (start us, length us, event | category | flops | bytes accessed | tf_op | source)
XLA Modules:
  0.0 68.4 jit_solution(6103907405588691287)
XLA Ops:
  0.0 29.2 %spread.1 = (f32[4,32,1024]{2,1,0:T(8,128)}, f32[2,4,32,1024]{3,2,1,0:T(8,128)}, f32[32,1024]{1,0:T(8,128)}, f32[2,8,1024]{2,1,0:T(8,128)}) custom-call(s32[2]{0:T(128)} %owner_ref.1, f32[4]{0:T(128)} %shift_ref.1, s32[4]{0:T(128)} %weight_ref.1, f32[2,4,16,1024]{3,2,1,0:T(8,128)} %bitcast.3, f32[4,16,1024]{2,1,0:T(8,128)} %orb_ref.1, f32[16,1024]{1,0:T(8,128)} %local_ref.1), custom_call_target="tpu_custom_call" | custom-call | tf_op jit(solution)/shard_map/spread/pallas_call | solution.py:466
  29.2 12.2 %sweeps.1.part_ref = f32[4,16,1024]{2,1,0:T(8,128)} custom-call(f32[2,8,1024]{2,1,0:T(8,128)} %get-tuple-element.9.pack_ref, f32[4,32,1024]{2,1,0:T(8,128)} %get-tuple-element.10.trial_ref, f32[2,4,32,1024]{3,2,1,0:T(8,128)} %get-tuple-element.11.orb_ref, f32[32,1024]{1,0:T(8,128)} %get-tuple-element.12.local_ref), custom_call_target="tpu_custom_call" | custom-call | tf_op jit(solution)/shard_map/sweeps/pallas_call | solution.py:486
  41.4 24.4 %total.1 = f32[2,4,16,1024]{3,2,1,0:T(8,128)} custom-call(f32[4,16,1024]{2,1,0:T(8,128)} %sweeps.1.part_ref), custom_call_target="tpu_custom_call" | custom-call | tf_op jit(solution)/shard_map/total/pallas_call | solution.py:504
  65.8 0.0 copy-start
  65.8 0.6 copy-done
  66.4 2.0 %select_bitcast_fusion = f32[1,2,4,16,1024]{4,3,2,1,0:T(8,128)} fusion(f32[2,4,16,1024]{3,2,1,0:T(8,128)} %total.1, pred[2]{0:T(512)(128)(4,1)S(1)} %broadcast_compare_fusion), kind=kLoop, calls=%fused_computation | loop fusion | flops 131072 | bytes 1048578 | tf_op jit(solution)/shard_map/broadcast_in_dim | solution.py:514
  (1 shorter events, 0.0 us)
Async XLA Ops:
  65.8 0.7 copy-start

commit v4 on v3

--- a/solution.py
+++ b/solution.py
@@ -77,7 +77,7 @@
     )
 
 
-LAG = 2
+LAG = 4
 
 
 class Waves:
@@ -450,6 +450,11 @@
             out_ref[:, x, :] = density[x, 0:half] + density[x, half:batch]
 
 
+def own_kernel(owner_ref, total_ref, out_ref):
+    for b in range(total_ref.shape[0]):
+        out_ref[b] = jnp.where(owner_ref[b] == lax.axis_index("orb"), total_ref[b], 0.0)
+
+
 def shards(count, grids, potentials, orbitals, local_pot, shifts, occupation, owner):
     _, blocks, kinds, rows, cells = potentials.shape
     batch = blocks * kinds
@@ -510,8 +515,14 @@
         compiler_params=pltpu.CompilerParams(collective_id=1, has_side_effects=True),
         name="total",
     )(partial)
-    owned = (owner == lax.axis_index("orb"))[:, None, None, None]
-    return jnp.where(owned, totals.reshape(blocks, kinds, rows, cells), 0.0)[None]
+    response = pl.pallas_call(
+        own_kernel,
+        out_shape=jax.ShapeDtypeStruct((blocks, kinds, rows, cells), f32),
+        in_specs=[smem, vmem],
+        out_specs=vmem,
+        name="own",
+    )(owner, totals.reshape(blocks, kinds, rows, cells))
+    return response[None]
 
 
 def solution(mesh):

time: 69.5 us -> 60.5 us (0.87); the launches traced: 68.4 us -> 60.3 us
  Pallas kernels: 65.8 us -> 60.3 us
  other arithmetic: 1.96 us -> 0 us
    pallas_call x1, Pallas kernels: 24.4 us -> 20.6 us  [shards(): pl.pallas_call(functools.partial(total_kernel, count, grids), out_shape=j...]
    pallas_call x1, Pallas kernels: 29.2 us -> 25.5 us  [shards(): pl.pallas_call(functools.partial(spread_kernel, count, grids, kinds), out...]
    broadcast_in_dim x1 -> x0, other arithmetic: 1.95 us -> none  [shards(): jnp.where(owned, totals.reshape(blocks, kinds, rows, cells), 0.0)[None]]
    pallas_call x0 -> x1, Pallas kernels: none -> 1.89 us  [shards(): pl.pallas_call(own_kernel, out_shape=jax.ShapeDtypeStruct((blocks, kinds,...]
where the time goes in v4:
time: 60.5 us; the launch traced here: 60.3 us
  Pallas kernels  60.3 us (100%)
    pallas_call x1, Pallas kernels, shards(): pl.pallas_call(functools.partial(spread_kernel, count, grids, kinds), out...  25.5 us
    pallas_call x1, Pallas kernels, shards(): pl.pallas_call(functools.partial(total_kernel, count, grids), out_shape=j...  20.6 us
    pallas_call x1, Pallas kernels, shards(): pl.pallas_call(functools.partial(sweep_kernel, grids), out_shape=jax.Shap...  12.2 us
    pallas_call x1, Pallas kernels, shards(): pl.pallas_call(own_kernel, out_shape=jax.ShapeDtypeStruct((blocks, kinds,...  1.89 us

profile of v4, /device:TPU:0, one launch (start us, length us, event | category | flops | bytes accessed | tf_op | source)
XLA Modules:
  0.0 60.3 jit_solution(4177454036011418584)
XLA Ops:
  0.0 25.5 %spread.1 = (f32[4,32,1024]{2,1,0:T(8,128)}, f32[2,4,32,1024]{3,2,1,0:T(8,128)}, f32[32,1024]{1,0:T(8,128)}, f32[2,8,1024]{2,1,0:T(8,128)}) custom-call(s32[2]{0:T(128)} %owner_ref.3, f32[4]{0:T(128)} %shift_ref.1, s32[4]{0:T(128)} %weight_ref.1, f32[2,4,16,1024]{3,2,1,0:T(8,128)} %bitcast.2, f32[4,16,1024]{2,1,0:T(8,128)} %orb_ref.1, f32[16,1024]{1,0:T(8,128)} %local_ref.1), custom_call_target="tpu_custom_call" | custom-call | tf_op jit(solution)/shard_map/spread/pallas_call | solution.py:471
  25.6 12.2 %sweeps.1.part_ref = f32[4,16,1024]{2,1,0:T(8,128)} custom-call(f32[2,8,1024]{2,1,0:T(8,128)} %get-tuple-element.9.pack_ref, f32[4,32,1024]{2,1,0:T(8,128)} %get-tuple-element.10.trial_ref, f32[2,4,32,1024]{3,2,1,0:T(8,128)} %get-tuple-element.11.orb_ref, f32[32,1024]{1,0:T(8,128)} %get-tuple-element.12.local_ref), custom_call_target="tpu_custom_call" | custom-call | tf_op jit(solution)/shard_map/sweeps/pallas_call | solution.py:491
  37.8 20.6 %total.1.total_ref = f32[2,4,16,1024]{3,2,1,0:T(8,128)} custom-call(f32[4,16,1024]{2,1,0:T(8,128)} %sweeps.1.part_ref), custom_call_target="tpu_custom_call" | custom-call | tf_op jit(solution)/shard_map/total/pallas_call | solution.py:509
  58.4 1.9 %own.1 = f32[2,4,16,1024]{3,2,1,0:T(8,128)} custom-call(s32[2]{0:T(128)} %owner_ref.3, f32[2,4,16,1024]{3,2,1,0:T(8,128)} %total.1.total_ref), custom_call_target="tpu_custom_call" | custom-call | tf_op jit(solution)/shard_map/own/pallas_call | solution.py:518
